TPU v7x, 512 devices: a whole 4x8x8 slice. The times are simulated.
512 devices in a mesh: seq: 64 (over z, x, core), head: 8 (over y).
Axes of the slice: x: 4, y: 8, z: 8, core: 2. Of those that a mesh axis runs over, the one named last changes fastest.
Arguments:
- queries: bfloat16 [65536, 3072], P('seq', 'head'), may hold values from -6 to 6
- keys: bfloat16 [65536, 3072], P('seq', 'head'), may hold values from -6 to 6
- values: bfloat16 [65536, 3072], P('seq', 'head'), may hold values from -6 to 6
- tile_pool: int32 [24, 1024], P('head'), may hold values from 0 to 511, as said below
- tile_lists: int32 [24, 512, 12], P('head', 'seq'), may hold values from 0 to 15, as said below
- key_slot: int32 [512], replicated, may hold values from 0 to 511, as said below
Outputs:
- attended: bfloat16 [65536, 3072], P(('seq', 'head'))
Inputs may be any that keep to these rules, and one draw needn't show every extreme that they name: `tile_pool`: for each index i of seq and each group of 3 heads (heads g * 3 onward), the pool entries of those heads for index i (columns i * 16 onward) name tiles whose slots lie on any one index of seq (slot // 8) at most 1 times, and exactly 1 times on some index. `tile_lists`: the 12 entries of one head and one query tile are distinct. `key_slot`: A permutation of the tiles that keeps tiles 0 to 3 at their own slots.
All inputs are finite; a program needn't handle non-finite values.
Results may differ from a plain program's by a relative error of at most 0.0043.
Values may be sent and summed in bfloat16 or wider, within the bound.
A program may use at most 64 MiB of HBM per device.

v0:
```python
import jax
import jax.numpy as jnp
from jax import lax
from jax.sharding import PartitionSpec as P

TILE = 128
SHARED = 4


def from_root(value, axis, source):
    kept = jnp.where(lax.axis_index(axis) == source, value, 0).astype(value.dtype)
    return lax.psum(kept, axis)


def arrange(matrix, tile_count, head_count, head_size):
    return matrix.reshape(tile_count, TILE, head_count, head_size).transpose(2, 0, 1, 3)


def finish(scores, value_part, pattern):
    tile_top = jnp.max(scores, -1)
    weights = jnp.exp(scores - tile_top[..., None])
    row_total = jnp.sum(weights, -1)
    numerator = jnp.einsum(
        pattern, weights.astype(jnp.bfloat16), value_part, preferred_element_type=jnp.float32
    )
    return (numerator, tile_top, row_total)


def blend_tiles(numerator, tile_top, row_total):
    overall = jnp.max(tile_top, 1, keepdims=True)
    factor = jnp.exp(tile_top - overall)
    upper = jnp.sum(factor[..., None] * numerator, 1)
    lower = jnp.sum(factor * row_total, 1)
    return (upper / lower[..., None]).astype(jnp.bfloat16)


def body(queries, keys, values, tile_pool, tile_lists, key_slot):
    seq_count = lax.axis_size("seq")
    my_index = lax.axis_index("seq")
    head_count, pool_total = tile_pool.shape
    pool_len = pool_total // seq_count
    list_len = tile_lists.shape[2]
    rows, width = queries.shape
    head_size = width // head_count
    tile_count = rows // TILE
    bound_slots = (head_count * pool_len + seq_count - 1) // seq_count
    block_tiles = min(tile_count, max(1, 512 // TILE))
    block_count = tile_count // block_tiles
    scaling = head_size ** (-0.5)
    query_heads = arrange(queries, tile_count, head_count, head_size)
    key_value = jnp.concatenate(
        [
            arrange(keys, tile_count, head_count, head_size),
            arrange(values, tile_count, head_count, head_size),
        ],
        -1,
    )
    flat_kv = key_value.reshape(head_count * tile_count, TILE, 2 * head_size)
    shared = from_root(key_value[:, :SHARED], "seq", 0)
    own_pool = lax.dynamic_slice_in_dim(tile_pool, my_index * pool_len, pool_len, 1)
    storage = key_slot[own_pool]
    owner_dev = (storage // tile_count).reshape(-1)
    head_ids = jnp.arange(head_count, dtype=jnp.int32)[:, None]
    req_code = (head_ids * tile_count + storage % tile_count).reshape(-1)
    matches = (owner_dev[:, None] == jnp.arange(seq_count, dtype=jnp.int32)[None, :]).astype(
        jnp.int32
    )
    slot_pos = jnp.sum((jnp.cumsum(matches, 0) - matches) * matches, 1)
    owner_dev, slot_pos, req_code = (owner_dev, slot_pos, req_code)
    outgoing = jnp.zeros((seq_count, bound_slots), jnp.int32).at[owner_dev, slot_pos].set(req_code)
    incoming = lax.all_to_all(outgoing, "seq", split_axis=0, concat_axis=0, tiled=True)
    replies = lax.all_to_all(flat_kv[incoming], "seq", split_axis=0, concat_axis=0, tiled=True)
    pool_tiles = replies[
        owner_dev.reshape(head_count, pool_len), slot_pos.reshape(head_count, pool_len)
    ]
    query_blocks = query_heads.reshape(head_count * block_count, block_tiles, TILE, head_size)
    list_blocks = tile_lists.reshape(head_count * block_count, block_tiles, list_len)
    head_of = jnp.arange(head_count * block_count, dtype=jnp.int32) // block_count

    def per_block(member):
        query_blk, list_blk, head_id = member
        listed = pool_tiles[head_id][list_blk]
        shared_head = shared[head_id]
        common = jnp.broadcast_to(shared_head[None], (block_tiles,) + shared_head.shape)
        keyset = jnp.concatenate([common, listed], 1)
        scores = (
            jnp.einsum(
                "tqd,tjkd->tjqk",
                query_blk,
                keyset[..., :head_size],
                preferred_element_type=jnp.float32,
            )
            * scaling
        )
        numerator, tile_top, row_total = finish(scores, keyset[..., head_size:], "tjqk,tjkd->tjqd")
        return blend_tiles(numerator, tile_top, row_total)

    per_blocks = lax.map(per_block, (query_blocks, list_blocks, head_of))
    per_heads = per_blocks.reshape(head_count, tile_count, TILE, head_size)
    result = per_heads.transpose(1, 2, 0, 3).reshape(rows, width)
    return lax.all_to_all(result, "head", split_axis=0, concat_axis=1, tiled=True)


def solution(mesh):
    return jax.shard_map(
        body,
        mesh=mesh,
        in_specs=(
            P("seq", "head"),
            P("seq", "head"),
            P("seq", "head"),
            P("head", None),
            P("head", "seq", None),
            P(),
        ),
        out_specs=P(("seq", "head"), None),
        check_vma=False,
    )
```

profile of v0, /device:TPU:2, one launch (start us, length us, event | category | flops | bytes accessed | tf_op | source)
XLA Modules:
  0.0 390.8 jit_solution(4417109201509644880)
XLA Ops:
  10.2 13.9 %all-to-all-start = ((s32[64,1,1]{2,1,0:T(1,128)}), s32[64,1,1]{2,1,0:T(1,128)S(1)}, u32[]{:S(2)}, u32[]{:S(2)}) async-start(s32[64,1,1]{2,1,0:T(1,128)} %copy.50), calls=%async_computation | async-start | bytes 65536 | tf_op jit(solution)/shard_map/all_to_all | solution.py:71
  24.1 1.4 copy.47
  26.2 1.3 pad_maximum_fusion.2
  27.5 2.2 copy.49
  29.7 3.0 all-to-all-done
  32.6 1.2 fusion.20
  33.9 2.8 gather_fusion.2
  36.7 7.7 %all-to-all-start.1 = ((bf16[64,1,128,256]{3,2,1,0:T(8,128)(2,1)}), bf16[64,1,128,256]{3,2,1,0:T(8,128)(2,1)}, u32[]{:S(2)}, u32[]{:S(2)}) async-start(bf16[64,1,128,256]{3,2,1,0:T(8,128)(2,1)} %bitcast.115), calls=%async_computation.1 | async-start | bytes 8388608 | tf_op jit(solution)/shard_map/all_to_all | solution.py:72
  44.4 1.3 fusion.19
  47.0 96.1 %all-to-all-done.1 = bf16[64,1,128,256]{3,2,1,0:T(8,128)(2,1)} async-done(((bf16[64,1,128,256]{3,2,1,0:T(8,128)(2,1)}), bf16[64,1,128,256]{3,2,1,0:T(8,128)(2,1)}, u32[]{:S(2)}, u32[]{:S(2)}) %all-to-all-start.1) | async-done | bytes 4194336 | tf_op jit(solution)/shard_map/all_to_all | solution.py:72
  143.1 4.7 %gather_fusion.3 = bf16[48,128,256]{2,1,0:T(8,128)(2,1)} fusion(bf16[64,1,128,256]{3,2,1,0:T(8,128)(2,1)} %all-to-all-done.1, s32[48]{0:T(128)S(1)} %reshape.314), kind=kCustom, calls=%fused_computation.3 | custom fusion | bytes 6291840 | tf_op jit(solution)/shard_map/gather | solution.py:73
  147.8 115.8 %all-reduce.2.cloned.1.call-done = bf16[3,4,128,256]{2,1,3,0:T(4,128)(2,1)} async-done(((bf16[3,4,128,256]{2,1,3,0:T(4,128)(2,1)}), bf16[3,4,128,256]{2,1,3,0:T(4,128)(2,1)}) %all-reduce.2.cloned.1.call-update) | async-done | bytes 786448 | tf_op jit(solution)/shard_map/psum | solution.py:12
  263.6 89.6 %while.10 = (s32[]{:T(128)}, bf16[6,4,128,128]{3,2,1,0:T(8,128)(2,1)S(1)}, s32[6]{0:T(128)S(1)}, bf16[3,4,128,256]{2,1,3,0:T(4,128)(2,1)}, bf16[3,16,128,256]{3,...) while((s32[]{:T(128)}, ...), condition=%wide.region_10.11_spmd, body=%wide.region_4.10_spmd.sunk | while | flops 553721984 | bytes 45364548 | solution.py:98
  266.1 1.3 dynamic-slice_bitcast_fusion.2
  268.2 2.5 gather_fusion
  270.7 1.0 constant_dynamic-slice_fusion.2
  272.1 2.1 bitcast_reduce_fusion.3
  274.2 1.3 fusion.37
  276.1 2.2 multiply_reduce_fusion.5
  281.1 1.3 dynamic-slice_bitcast_fusion.2
  283.1 2.5 gather_fusion
  285.7 1.0 constant_dynamic-slice_fusion.2
  287.0 2.1 bitcast_reduce_fusion.3
  289.2 1.3 fusion.37
  291.0 2.2 multiply_reduce_fusion.5
  296.0 1.3 dynamic-slice_bitcast_fusion.2
  298.1 2.5 gather_fusion
  300.6 1.0 constant_dynamic-slice_fusion.2
  301.9 2.1 bitcast_reduce_fusion.3
  304.1 1.3 fusion.37
  306.0 2.2 multiply_reduce_fusion.5
  310.9 1.3 dynamic-slice_bitcast_fusion.2
  313.0 2.5 gather_fusion
  316.9 2.1 bitcast_reduce_fusion.3
  319.0 1.3 fusion.37
  320.9 2.2 multiply_reduce_fusion.5
  325.9 1.3 dynamic-slice_bitcast_fusion.2
  328.0 2.5 gather_fusion
  331.8 2.1 bitcast_reduce_fusion.3
  334.0 1.3 fusion.37
  335.9 2.2 multiply_reduce_fusion.5
  340.8 1.3 dynamic-slice_bitcast_fusion.2
  342.9 2.5 gather_fusion
  346.8 2.1 bitcast_reduce_fusion.3
  348.9 1.3 fusion.37
  350.8 2.2 multiply_reduce_fusion.5
  354.0 28.4 %all_to_all.33 = bf16[8,128,384]{2,1,0:T(8,128)(2,1)S(1)} all-to-all(bf16[8,128,384]{2,1,0:T(8,128)(2,1)S(1)} %copy.56), channel_id=1, replica_groups=mesh['seq'=64,'head'=8] {'head'}, dimensions={0} | all-to-all | bytes 1572864 | tf_op jit(solution)/shard_map/all_to_all | solution.py:101
  382.8 1.2 copy.58
  (101 shorter events, 24.4 us)
Async XLA Ops:
  6.5 1.1 copy-start
  6.5 19.2 %copy-start.2 = (bf16[1024,384]{1,0:T(8,128)(2,1)S(1)}, bf16[1024,384]{1,0:T(8,128)(2,1)}, u32[]{:S(2)}) copy-start(bf16[1024,384]{1,0:T(8,128)(2,1)} %param.10) | copy-start | bytes 2359300
  10.2 22.4 %all-to-all-start = ((s32[64,1,1]{2,1,0:T(1,128)}), s32[64,1,1]{2,1,0:T(1,128)S(1)}, u32[]{:S(2)}, u32[]{:S(2)}) async-start(s32[64,1,1]{2,1,0:T(1,128)} %copy.50), calls=%async_computation | async-start | bytes 65536 | tf_op jit(solution)/shard_map/all_to_all | solution.py:71
  36.7 9.3 %copy-start.3 = (bf16[1024,384]{1,0:T(8,128)(2,1)S(1)}, bf16[1024,384]{1,0:T(8,128)(2,1)}, u32[]{:S(2)}) copy-start(bf16[1024,384]{1,0:T(8,128)(2,1)} %param.8) | copy-start | bytes 2359300
  36.7 106.4 %all-to-all-start.1 = ((bf16[64,1,128,256]{3,2,1,0:T(8,128)(2,1)}), bf16[64,1,128,256]{3,2,1,0:T(8,128)(2,1)}, u32[]{:S(2)}, u32[]{:S(2)}) async-start(bf16[64,1,128,256]{3,2,1,0:T(8,128)(2,1)} %bitcast.115), calls=%async_computation.1 | async-start | bytes 8388608 | tf_op jit(solution)/shard_map/all_to_all | solution.py:72
  44.3 219.3 %all-reduce.2.cloned.1.call-start = ((), (), s32[]{:S(2)}) async-start(), calls=%async_computation.3 | async-start | bytes 1572864 | tf_op jit(solution)/shard_map/psum | solution.py:12
  274.2 1.9 copy-start.1
  289.1 1.9 copy-start.1
  304.1 1.9 copy-start.1
  319.0 1.9 copy-start.1
  334.0 1.9 copy-start.1
  348.9 1.9 copy-start.1
Sparse Core Ops, SparseCore 0:
  48.6 214.9 all-reduce.1
where the time goes:
time: 392 us; the launch traced here: 391 us
  waiting for transfers between devices  215 us (55%)
  local copies, waits for them, and re-layouts  55.9 us (14%)
  blocking collectives  28.4 us (7%)
  matrix products  26.3 us (7%)
  starting transfers between devices  21.6 us (6%)
  other arithmetic  18.2 us (5%)
  between operations  13.6 us (3%)
  loops' own time  12.1 us (3%)
    psum x1, waiting for transfers between devices, from_root(): return lax.psum(kept, axis)  116 us
    all_to_all x1, waiting for transfers between devices, body(): lax.all_to_all(flat_kv[incoming], 'seq', split_axis=0, concat_axis=0, til...  96.1 us
    all_to_all x1, blocking collectives, body(): lax.all_to_all(result, 'head', split_axis=0, concat_axis=1, tiled=True)  28.4 us
    gather x6, local copies, waits for them, and re-layouts, per_block(): listed = pool_tiles[head_id][list_blk]  15.1 us
    all_to_all x1, starting transfers between devices, body(): lax.all_to_all(outgoing, 'seq', split_axis=0, concat_axis=0, tiled=True)  13.9 us
    dot_general x6, matrix products, finish(): jnp.einsum(pattern, weights.astype(jnp.bfloat16), value_part, preferred_e...  13.4 us
    dot_general x6, matrix products, per_block(): jnp.einsum('tqd,tjkd->tjqk', query_blk, keyset[..., :head_size], preferre...  12.9 us
    another operation x1, loops' own time, body(): per_blocks = lax.map(per_block, (query_blocks, list_blocks, head_of))  12.1 us
  transfers between devices with their start and end apart: 3, of which 3 were waited for; matrix products, arithmetic and copies ran while one was open for 3% of the time, Pallas kernels for 0%

commit v1 on v0

--- a/solution.py
+++ b/solution.py
@@ -9,7 +9,7 @@
 
 def from_root(value, axis, source):
     kept = jnp.where(lax.axis_index(axis) == source, value, 0).astype(value.dtype)
-    return lax.psum(kept, axis)
+    return jnp.sum(lax.all_gather(kept, axis), axis=0)
 
 
 def arrange(matrix, tile_count, head_count, head_size):

time: 392 us -> 421 us (1.074)
  the two profiles are of different devices: /device:TPU:2 before, /device:TPU:1 now
where the time goes in v1:
time: 421 us; the launch traced here: 420 us
  waiting for transfers between devices  232 us (55%)
  local copies, waits for them, and re-layouts  51.7 us (12%)
  other arithmetic  36.2 us (9%)
  blocking collectives  29.4 us (7%)
  matrix products  26.3 us (6%)
  starting transfers between devices  20.7 us (5%)
  between operations  13.6 us (3%)
  loops' own time  10.1 us (2%)
    all_to_all x1, waiting for transfers between devices, body(): lax.all_to_all(flat_kv[incoming], 'seq', split_axis=0, concat_axis=0, til...  121 us
    all_gather x1, waiting for transfers between devices, from_root(): return jnp.sum(lax.all_gather(kept, axis), axis=0)  103 us
    all_to_all x1, blocking collectives, body(): lax.all_to_all(result, 'head', split_axis=0, concat_axis=1, tiled=True)  29.4 us
    reduce_sum x1, other arithmetic, from_root(): return jnp.sum(lax.all_gather(kept, axis), axis=0)  16.2 us
    gather x6, local copies, waits for them, and re-layouts, per_block(): listed = pool_tiles[head_id][list_blk]  15.1 us
    all_to_all x1, starting transfers between devices, body(): lax.all_to_all(outgoing, 'seq', split_axis=0, concat_axis=0, tiled=True)  14.8 us
    dot_general x6, matrix products, finish(): jnp.einsum(pattern, weights.astype(jnp.bfloat16), value_part, preferred_e...  13.5 us
    dot_general x6, matrix products, per_block(): jnp.einsum('tqd,tjkd->tjqk', query_blk, keyset[..., :head_size], preferre...  12.8 us
  transfers between devices with their start and end apart: 3, of which 3 were waited for; matrix products, arithmetic and copies ran while one was open for 4% of the time, Pallas kernels for 0%

profile of v1, /device:TPU:1, one launch (start us, length us, event | category | flops | bytes accessed | tf_op | source)
XLA Modules:
  0.0 420.0 jit_solution(99563513658989438)
XLA Ops:
  6.5 1.4 copy.48
  8.1 1.4 copy.49
  10.1 1.2 copy.50
  14.9 14.8 %all-to-all-start = ((s32[64,1,1]{2,1,0:T(1,128)}), s32[64,1,1]{2,1,0:T(1,128)S(1)}, u32[]{:S(2)}, u32[]{:S(2)}) async-start(s32[64,1,1]{2,1,0:T(1,128)} %copy.52), calls=%async_computation | async-start | bytes 65536 | tf_op jit(solution)/shard_map/all_to_all | solution.py:71
  29.9 1.1 copy.51
  31.1 8.0 %all-to-all-done = s32[64,1,1]{2,1,0:T(1,128)S(1)} async-done(((s32[64,1,1]{2,1,0:T(1,128)}), s32[64,1,1]{2,1,0:T(1,128)S(1)}, u32[]{:S(2)}, u32[]{:S(2)}) %all-to-all-start) | async-done | bytes 288 | tf_op jit(solution)/shard_map/all_to_all | solution.py:71
  39.1 1.2 fusion.20
  40.3 2.8 gather_fusion.2
  43.1 5.8 %all-to-all-start.1 = ((bf16[64,1,128,256]{3,2,1,0:T(8,128)(2,1)}), bf16[64,1,128,256]{3,2,1,0:T(8,128)(2,1)}, u32[]{:S(2)}, u32[]{:S(2)}) async-start(bf16[64,1,128,256]{3,2,1,0:T(8,128)(2,1)} %bitcast.117), calls=%async_computation.1 | async-start | bytes 8388608 | tf_op jit(solution)/shard_map/all_to_all | solution.py:72
  49.7 1.4 copy.55
  51.1 120.9 %all-to-all-done.1 = bf16[64,1,128,256]{3,2,1,0:T(8,128)(2,1)} async-done(((bf16[64,1,128,256]{3,2,1,0:T(8,128)(2,1)}), bf16[64,1,128,256]{3,2,1,0:T(8,128)(2,1)}, u32[]{:S(2)}, u32[]{:S(2)}) %all-to-all-start.1) | async-done | bytes 4194336 | tf_op jit(solution)/shard_map/all_to_all | solution.py:72
  172.0 4.8 %gather_fusion.3 = bf16[48,128,256]{2,1,0:T(8,128)(2,1)} fusion(bf16[64,1,128,256]{3,2,1,0:T(8,128)(2,1)} %all-to-all-done.1, s32[48]{0:T(128)S(1)} %reshape.314), kind=kCustom, calls=%fused_computation.3 | custom fusion | bytes 6291840 | tf_op jit(solution)/shard_map/gather | solution.py:73
  176.7 103.0 %all-gather.3.cloned.1.call-done = bf16[192,4,128,256]{3,2,1,0:T(8,128)(2,1)} async-done(((bf16[3,4,128,256]{3,2,1,0:T(8,128)(2,1)}), bf16[192,4,128,256]{3,2,1,0:T(8,128)(2,1)}) %all-gather.3.cloned.1.call-update) | async-done | bytes 50331664 | tf_op jit(solution)/shard_map/all_gather | solution.py:12
  279.8 16.2 %reduce_sum.52 = bf16[3,4,128,256]{3,2,1,0:T(8,128)(2,1)S(1)} reduce(bf16[64,3,4,128,256]{4,3,2,1,0:T(8,128)(2,1)} %bitcast.114, bf16[]{:T(256)} %constant.84.clone.1), dimensions={0}, to_apply=%region_3.4 | reduce | flops 24772608 | bytes 51118080 | tf_op jit(solution)/shard_map/reduce_sum | solution.py:12
  296.0 84.2 %while.10 = (s32[]{:T(128)}, bf16[6,4,128,128]{3,2,1,0:T(8,128)(2,1)}, s32[6]{0:T(128)S(1)}, bf16[3,4,128,256]{3,2,1,0:T(8,128)(2,1)S(1)}, bf16[3,16,128,256]{3,...) while((s32[]{:T(128)}, ...), condition=%wide.region_10.11_spmd, body=%wide.region_4.10_spmd.sunk | while | flops 553721984 | bytes 44840268 | solution.py:98
  298.3 1.3 dynamic-slice_bitcast_fusion.5
  300.4 2.5 gather_fusion
  303.0 2.1 bitcast_reduce_fusion.3
  305.1 1.3 fusion.37
  307.0 2.3 multiply_reduce_fusion.5
  312.4 1.3 dynamic-slice_bitcast_fusion.5
  314.5 2.5 gather_fusion
  317.0 2.1 bitcast_reduce_fusion.3
  319.1 1.3 fusion.37
  321.0 2.3 multiply_reduce_fusion.5
  326.4 1.3 dynamic-slice_bitcast_fusion.5
  328.5 2.5 gather_fusion
  331.0 2.1 bitcast_reduce_fusion.3
  333.2 1.3 fusion.37
  335.1 2.3 multiply_reduce_fusion.5
  340.5 1.3 dynamic-slice_bitcast_fusion.5
  342.5 2.5 gather_fusion
  345.1 2.1 bitcast_reduce_fusion.3
  347.2 1.3 fusion.37
  349.1 2.3 multiply_reduce_fusion.5
  354.5 1.3 dynamic-slice_bitcast_fusion.5
  356.6 2.5 gather_fusion
  359.1 2.1 bitcast_reduce_fusion.3
  361.3 1.3 fusion.37
  363.1 2.3 multiply_reduce_fusion.5
  368.5 1.3 dynamic-slice_bitcast_fusion.5
  370.6 2.5 gather_fusion
  373.1 2.1 bitcast_reduce_fusion.3
  375.3 1.3 fusion.37
  377.2 2.3 multiply_reduce_fusion.5
  380.2 1.5 copy.56
  382.1 29.4 %all_to_all.33 = bf16[8,128,384]{2,1,0:T(8,128)(2,1)S(1)} all-to-all(bf16[8,128,384]{2,1,0:T(8,128)(2,1)S(1)} %copy.57), channel_id=1, replica_groups=mesh['seq'=64,'head'=8] {'head'}, dimensions={0} | all-to-all | bytes 1572864 | tf_op jit(solution)/shard_map/all_to_all | solution.py:101
  411.9 1.2 copy.59
  (97 shorter events, 22.8 us)
Async XLA Ops:
  6.5 5.8 %copy-start = (s32[512]{0:T(512)S(1)}, s32[512]{0:T(512)}, u32[]{:S(2)}) copy-start(s32[512]{0:T(512)} %param.13) | copy-start | bytes 6148
  6.5 273.2 %all-gather.3.cloned.1.call-start = ((), (), s32[]{:S(2)}) async-start(), calls=%async_computation.3 | async-start | bytes 51118080 | tf_op jit(solution)/shard_map/all_gather | solution.py:12
  14.9 24.2 %all-to-all-start = ((s32[64,1,1]{2,1,0:T(1,128)}), s32[64,1,1]{2,1,0:T(1,128)S(1)}, u32[]{:S(2)}, u32[]{:S(2)}) async-start(s32[64,1,1]{2,1,0:T(1,128)} %copy.52), calls=%async_computation | async-start | bytes 65536 | tf_op jit(solution)/shard_map/all_to_all | solution.py:71
  43.1 6.1 %copy-start.3 = (bf16[1024,384]{1,0:T(8,128)(2,1)S(1)}, bf16[1024,384]{1,0:T(8,128)(2,1)}, u32[]{:S(2)}) copy-start(bf16[1024,384]{1,0:T(8,128)(2,1)} %param.8) | copy-start | bytes 2359300
  43.1 128.9 %all-to-all-start.1 = ((bf16[64,1,128,256]{3,2,1,0:T(8,128)(2,1)}), bf16[64,1,128,256]{3,2,1,0:T(8,128)(2,1)}, u32[]{:S(2)}, u32[]{:S(2)}) async-start(bf16[64,1,128,256]{3,2,1,0:T(8,128)(2,1)} %bitcast.117), calls=%async_computation.1 | async-start | bytes 8388608 | tf_op jit(solution)/shard_map/all_to_all | solution.py:72
  305.1 1.9 copy-start.2
  319.1 1.9 copy-start.2
  333.2 1.9 copy-start.2
  347.2 1.9 copy-start.2
  361.2 1.9 copy-start.2
  375.3 1.9 copy-start.2
  380.2 32.9 %copy-start.1 = (s32[512]{0:T(512)S(1)}, s32[512]{0:T(512)}, u32[]{:S(2)}) copy-start(s32[512]{0:T(512)} %param.13) | copy-start | bytes 6148
Sparse Core Ops, SparseCore 0:
  11.4 268.2 all-gather.2
